TPU v7x, 256 devices: a whole 4x4x8 slice. The times are simulated.
256 devices in a mesh: front: 4 (over x), row: 8 (over z_hi, core), col: 8 (over y, z_lo).
Axes of the slice: x: 4, y: 4, z: 8 (z_hi: 4, z_lo: 2; z = z_hi * 2 + z_lo), core: 2. Of those that a mesh axis runs over, the one named last changes fastest.
Arguments:
- front: bfloat16 [4, 12288, 12288], P('front', 'row', 'col'), may hold values from -6 to 6
- panel: bfloat16 [4, 12288, 512], P('front', ('row', 'col')), may hold values from -8 to 8
- inverse: bfloat16 [4, 512, 512], P('front'), may hold values from -0.0046 to 0.056
- fill: int32 [4, 48], P('front'), may hold values 0 or 1
- block_map: int32 [4, 48], P('front'), may hold values from 0 to 47, as said below
- parent_front: bfloat16 [4, 6144, 12288], P('front', 'row', 'col'), may hold values from -6 to 6
Outputs:
- factor_rows: bfloat16 [4, 12288, 512], P('front', ('row', 'col'))
- parent: float32 [4, 6144, 12288], P('front', 'row', 'col')
Inputs may be any that keep to these rules, and one draw needn't show every extreme that they name: `block_map`: each front's map is a permutation of its blocks that keeps every aligned group of 6 blocks in place as a group.
All inputs are finite; a program needn't handle non-finite values. No bound on the sum of `fill` on one device may be relied on, other than what follows from the above.
Results may differ from a plain program's by a relative error of at most 0.0025.
Values may be sent and summed in bfloat16 or wider, within the bound.
A program may use at most 64 MiB of HBM per device.

v0:
```python
import jax
import jax.numpy as jnp
from jax import lax
from jax.sharding import PartitionSpec as P

BLK = 256


def from_partner(block, axis, distance):
    count = lax.axis_size(axis)
    route = []
    for low in range(count):
        high = low | 1 << distance
        if high != low and high < count:
            route += [(low, high), (high, low)]
    return lax.ppermute(block, axis, route)


def block_inverse(mapping, block_total):
    target = jnp.arange(block_total, dtype=jnp.int32)
    matches = (mapping[:, None] == target[None, :]).astype(jnp.int32)
    return jnp.sum(matches * target[:, None], axis=0)


def shards(front, panel, inverse, fill, block_map, parent_front):
    col_count = lax.axis_size("col")
    row_index = lax.axis_index("row")
    col_index = lax.axis_index("col")
    local_rows = panel.shape[1]
    tile_rows = front.shape[1]
    tile_cols = front.shape[2]
    block_total = fill.shape[1]
    first_row = (row_index * col_count + col_index) * local_rows
    positions = (first_row + jnp.arange(local_rows, dtype=jnp.int32)) // BLK
    blocks = jnp.arange(block_total, dtype=jnp.int32)
    row_fill = jnp.sum(
        (positions[:, None] == blocks[None, :]).astype(jnp.int32) * fill[0][None, :], axis=1
    )
    masked = panel[0] * row_fill[:, None].astype(jnp.bfloat16)
    factor = jnp.dot(masked, jnp.triu(inverse[0]), preferred_element_type=jnp.float32).astype(
        jnp.bfloat16
    )
    all_rows = lax.all_gather(factor, ("row", "col"), axis=0, tiled=True)
    row_side = lax.dynamic_slice_in_dim(all_rows, row_index * tile_rows, tile_rows, 0)
    col_side = lax.dynamic_slice_in_dim(all_rows, col_index * tile_cols, tile_cols, 0)
    contract = (((1,), (1,)), ((), ()))
    initial = front[0].astype(jnp.float32)
    row_blocks = tile_rows // BLK
    col_blocks = tile_cols // BLK
    update = lax.dot_general(row_side, col_side, contract, preferred_element_type=jnp.float32)
    schur = initial - update
    source = block_inverse(block_map[0], block_total)
    row_source = (
        lax.dynamic_slice_in_dim(source, row_index * row_blocks, row_blocks, 0)
        - row_index * row_blocks
    )
    col_source = (
        lax.dynamic_slice_in_dim(source, col_index * col_blocks, col_blocks, 0)
        - col_index * col_blocks
    )
    shaped = jnp.take(schur.reshape(row_blocks, BLK, tile_cols), row_source, axis=0)
    shaped = jnp.take(shaped.reshape(tile_rows, col_blocks, BLK), col_source, axis=1)
    contribution = shaped.reshape(tile_rows, tile_cols).astype(jnp.bfloat16)
    half_rows = tile_rows // 2
    parity = lax.axis_index("front") % 2
    kept_half = lax.dynamic_slice_in_dim(contribution, parity * half_rows, half_rows, 0)
    sent_half = lax.dynamic_slice_in_dim(contribution, (1 - parity) * half_rows, half_rows, 0)
    arrived = from_partner(sent_half, "front", 0)
    parent = (
        parent_front[0].astype(jnp.float32)
        + kept_half.astype(jnp.float32)
        + arrived.astype(jnp.float32)
    )
    return (factor[None], parent[None])


def solution(mesh):
    placed = (
        P("front", "row", "col"),
        P("front", ("row", "col"), None),
        P("front", None, None),
        P("front", None),
        P("front", None),
        P("front", "row", "col"),
    )
    return jax.shard_map(
        shards,
        mesh=mesh,
        in_specs=placed,
        out_specs=(P("front", ("row", "col"), None), P("front", "row", "col")),
        check_vma=False,
    )
```

profile of v0, /device:TPU:105, one launch (start us, length us, event | category | flops | bytes accessed | tf_op | source)
XLA Modules:
  0.0 335.8 jit_solution(6356897594682309380)
XLA Ops:
  7.2 0.0 all-gather.2.cloned.1.call-start
  7.2 0.7 select_reduce_fusion
  8.0 2.2 convolution_convert_fusion
  10.2 0.0 all-gather.2.cloned.1.call-update
  10.2 0.7 select_reduce_fusion.1
  11.0 0.1 compare_and_fusion.1
  11.1 0.1 broadcast_in_dim.52
  11.1 0.1 broadcast_in_dim.49
  11.3 204.7 %all-gather.2.cloned.1.call-done = bf16[12288,512]{1,0:T(8,128)(2,1)} async-done(((bf16[192,512]{1,0:T(8,128)(2,1)}), bf16[12288,512]{1,0:T(8,128)(2,1)}) %all-gather.2.cloned.1.call-update) | async-done | bytes 12582928 | tf_op jit(solution)/shard_map/all_gather | solution.py:43
  216.0 8.2 %convert_subtract_fusion = bf16[1536,1536]{1,0:T(8,128)(2,1)} fusion(bf16[1,1536,1536]{2,1,0:T(8,128)(2,1)} %param.6, bf16[12288,512]{1,0:T(8,128)(2,1)} %all-gather.2.cloned.1.call-done, s32[]{:T(128)S(6)} %select_n.68, s32[]{:T(128)S(6)} %select_n.67), kind=kOutput, calls=%fused_computation.2 | convolution fusion | flops 2422996992 | bytes 12582920 | tf_op jit(solution)/shard_map/dot_general | solution.py:50
  224.1 5.5 %gather_fusion = bf16[6,256,1536]{2,1,0:T(8,128)(2,1)} fusion(bf16[6,256,1536]{2,1,0:T(8,128)(2,1)} %bitcast.24, s32[1024]{0:T(1024)S(1)} %pad_clamp_fusion.1), kind=kCustom, calls=%fused_computation | custom fusion | bytes 9437208 | tf_op jit(solution)/shard_map/jit(_take)/gather | solution.py:61
  229.7 10.3 %gather.13 = bf16[1536,6,256]{2,1,0:T(8,128)(2,1)} reshape(bf16[6,256,1536]{2,1,0:T(8,128)(2,1)} %gather_fusion) | data formatting | bytes 9437184 | tf_op jit(solution)/shard_map/jit(_take)/gather | solution.py:61
  240.0 5.9 %copy_select_fusion = bf16[1536,6,256]{2,0,1:T(8,128)(2,1)} fusion(bf16[1536,6,256]{2,1,0:T(8,128)(2,1)} %gather.13, pred[1536]{0:T(1024)(128)(4,1)S(1)} %broadcast_in_dim.53), kind=kLoop, calls=%fused_computation.5 | loop fusion | flops 2359296 | bytes 9438720 | tf_op jit(solution)/shard_map/jit(_take)/select_n | solution.py:61
  245.8 5.5 %gather_fusion.1 = bf16[6,1536,256]{2,1,0:T(8,128)(2,1)} fusion(bf16[1536,6,256]{2,0,1:T(8,128)(2,1)} %copy_select_fusion, s32[1024]{0:T(1024)S(1)} %pad_clamp_fusion), kind=kCustom, calls=%fused_computation.1 | custom fusion | bytes 9437208 | tf_op jit(solution)/shard_map/jit(_take)/gather | solution.py:62
  251.3 6.6 %copy.14 = bf16[1536,6,256]{0,2,1:T(8,128)(2,1)} copy(bf16[1536,6,256]{2,0,1:T(8,128)(2,1)} %bitcast.23) | data formatting | bytes 9437184 | tf_op jit(solution)/shard_map/jit(_take)/gather | solution.py:62
  257.9 3.2 fusion
  261.1 0.0 copy-start
  261.1 2.2 copy-done
  263.3 1.6 constant_dynamic-slice_fusion
  264.8 1.2 collective-permute-start
  266.0 2.8 copy.12
  268.9 48.8 %collective-permute-done = bf16[768,1536]{0,1:T(8,128)(2,1)} collective-permute-done((bf16[768,1536]{0,1:T(8,128)(2,1)}, bf16[768,1536]{0,1:T(8,128)(2,1)}, u32[]{:S(2)}, u32[]{:S(2)}) %collective-permute-start) | collective-permute-done | bytes 2359328 | tf_op jit(solution)/shard_map/ppermute | solution.py:16
  317.6 5.3 %fusion.2 = f32[1,768,1536]{1,2,0:T(8,128)} fusion(bf16[768,1536]{0,1:T(8,128)(2,1)} %collective-permute-done, bf16[1,768,1536]{1,2,0:T(8,128)(2,1)S(1)} %copy.12, bf16[1536,1536]{0,1:T(8,128)(2,1)} %copy-done, s32[]{:T(128)S(6)} %select_n.72), kind=kLoop, calls=%fused_computation.8 | loop fusion | flops 5898240 | bytes 11796484 | tf_op jit(solution)/shard_map/broadcast_in_dim | solution.py:74
  322.9 6.0 %copy.15 = f32[1,768,1536]{2,1,0:T(8,128)} copy(f32[1,768,1536]{1,2,0:T(8,128)} %fusion.2) | data formatting | bytes 9437184
  (7 shorter events, 0.1 us)
Async XLA Ops:
  7.2 208.8 %all-gather.2.cloned.1.call-start = ((), (), s32[]{:S(2)}) async-start(), calls=%async_computation | async-start | bytes 12779520 | tf_op jit(solution)/shard_map/all_gather | solution.py:43
  261.1 2.2 copy-start
  264.8 52.8 %collective-permute-start = (bf16[768,1536]{0,1:T(8,128)(2,1)}, bf16[768,1536]{0,1:T(8,128)(2,1)}, u32[]{:S(2)}, u32[]{:S(2)}) collective-permute-start(bf16[768,1536]{0,1:T(8,128)(2,1)} %constant_dynamic-slice_fusion), channel_id=1, source_target_pairs={{0,64},{64,0},{128,192},{192,128},{1,65},{65,1},{129,193},{193,129... | collective-permute-start | bytes 7077896 | tf_op jit(solution)/shard_map/ppermute | solution.py:16
Sparse Core Ops, SparseCore 0:
  10.4 205.5 all-gather.1
where the time goes:
time: 337 us; the launch traced here: 336 us
  waiting for transfers between devices  253 us (75%)
  local copies, waits for them, and re-layouts  40.7 us (12%)
  other arithmetic  15.9 us (5%)
  between operations  14.1 us (4%)
  matrix products  10.4 us (3%)
    all_gather x1, waiting for transfers between devices, shards(): all_rows = lax.all_gather(factor, ('row', 'col'), axis=0, tiled=True)  205 us
    ppermute x1, waiting for transfers between devices, from_partner(): return lax.ppermute(block, axis, route)  48.8 us
    gather x2, local copies, waits for them, and re-layouts, shards(): jnp.take(schur.reshape(row_blocks, BLK, tile_cols), row_source, axis=0)  15.8 us
    gather x2, local copies, waits for them, and re-layouts, shards(): jnp.take(shaped.reshape(tile_rows, col_blocks, BLK), col_source, axis=1)  12.1 us
    unnamed x4, local copies, waits for them, and re-layouts  11.1 us
    dot_general x1, matrix products, shards(): lax.dot_general(row_side, col_side, contract, preferred_element_type=jnp....  8.18 us
  transfers between devices with their start and end apart: 2, of which 2 were waited for; matrix products, arithmetic and copies ran while one was open for 1% of the time, Pallas kernels for 0%

commit v1 on v0

--- a/solution.py
+++ b/solution.py
@@ -40,7 +40,10 @@
     factor = jnp.dot(masked, jnp.triu(inverse[0]), preferred_element_type=jnp.float32).astype(
         jnp.bfloat16
     )
-    all_rows = lax.all_gather(factor, ("row", "col"), axis=0, tiled=True)
+    all_rows = jnp.concatenate(
+        lax.all_to_all(jnp.stack([factor] * lax.axis_size(("row", "col"))), ("row", "col"), 0, 0),
+        axis=0,
+    )
     row_side = lax.dynamic_slice_in_dim(all_rows, row_index * tile_rows, tile_rows, 0)
     col_side = lax.dynamic_slice_in_dim(all_rows, col_index * tile_cols, tile_cols, 0)
     contract = (((1,), (1,)), ((), ()))

time: 337 us -> 413 us (1.23); the launches traced: 336 us -> 407 us
  waiting for transfers between devices: 253 us -> 322 us
  between operations: 14.1 us -> 0.76 us
  starting transfers between devices: 1.22 us -> 12.6 us
  local copies, waits for them, and re-layouts: 40.7 us -> 46.7 us
    all_to_all x0 -> x1, waiting for transfers between devices: none -> 273 us  [shards(): lax.all_to_all(jnp.stack([factor] * lax.axis_size(('row', 'col'))), ('row...]
    all_gather x1 -> x0, waiting for transfers between devices: 205 us -> none  [shards(): all_rows = lax.all_gather(factor, ('row', 'col'), axis=0, tiled=True)]
    all_to_all x0 -> x1, starting transfers between devices: none -> 11.4 us  [shards(): lax.all_to_all(jnp.stack([factor] * lax.axis_size(('row', 'col'))), ('row...]
    another operation x0 -> x1, local copies, waits for them, and re-layouts: none -> 5.99 us  [shards(): jnp.stack([factor] * lax.axis_size(('row', 'col')))]
    unnamed x4 -> x8, local copies, waits for them, and re-layouts: 11.1 us -> 11.1 us
where the time goes in v1:
time: 413 us; the launch traced here: 407 us
  waiting for transfers between devices  322 us (78%)
  local copies, waits for them, and re-layouts  46.7 us (11%)
  other arithmetic  15.2 us (4%)
  starting transfers between devices  12.6 us (3%)
  matrix products  9.63 us (2%)
    all_to_all x1, waiting for transfers between devices, shards(): lax.all_to_all(jnp.stack([factor] * lax.axis_size(('row', 'col'))), ('row...  273 us
    ppermute x1, waiting for transfers between devices, from_partner(): return lax.ppermute(block, axis, route)  48.3 us
    gather x2, local copies, waits for them, and re-layouts, shards(): jnp.take(schur.reshape(row_blocks, BLK, tile_cols), row_source, axis=0)  15.8 us
    gather x2, local copies, waits for them, and re-layouts, shards(): jnp.take(shaped.reshape(tile_rows, col_blocks, BLK), col_source, axis=1)  12.1 us
    all_to_all x1, starting transfers between devices, shards(): lax.all_to_all(jnp.stack([factor] * lax.axis_size(('row', 'col'))), ('row...  11.4 us
    unnamed x8, local copies, waits for them, and re-layouts  11.1 us
  transfers between devices with their start and end apart: 2, of which 2 were waited for; matrix products, arithmetic and copies ran while one was open for 1% of the time, Pallas kernels for 0%

profile of v1, /device:TPU:105, one launch (start us, length us, event | category | flops | bytes accessed | tf_op | source)
XLA Modules:
  0.0 406.6 jit_solution(563323751498706850)
XLA Ops:
  0.7 0.7 select_reduce_fusion
  1.4 1.5 convolution_convert_fusion
  2.9 0.0 copy-start.1
  2.9 6.0 %stack.2 = bf16[64,192,512]{2,1,0:T(8,128)(2,1)} broadcast(bf16[192,512]{1,0:T(8,128)(2,1)S(1)} %convolution_convert_fusion), dimensions={1,2} | broadcast | bytes 12779520 | tf_op jit(solution)/shard_map/stack | solution.py:44
  8.9 11.4 %all-to-all-start = ((bf16[64,192,512]{2,1,0:T(8,128)(2,1)}), bf16[64,192,512]{2,1,0:T(8,128)(2,1)}, u32[]{:S(2)}, u32[]{:S(2)}) async-start(bf16[64,192,512]{2,1,0:T(8,128)(2,1)} %stack.2), calls=%async_computation | async-start | bytes 25165824 | tf_op jit(solution)/shard_map/all_to_all | solution.py:44
  20.4 0.1 select_reduce_fusion.1
  20.4 0.1 compare_and_fusion.1
  20.5 0.1 broadcast_in_dim.52
  20.6 0.1 broadcast_in_dim.49
  20.7 273.4 %all-to-all-done = bf16[64,192,512]{2,1,0:T(8,128)(2,1)} async-done(((bf16[64,192,512]{2,1,0:T(8,128)(2,1)}), bf16[64,192,512]{2,1,0:T(8,128)(2,1)}, u32[]{:S(2)}, u32[]{:S(2)}) %all-to-all-start) | async-done | bytes 12582944 | tf_op jit(solution)/shard_map/all_to_all | solution.py:44
  294.1 8.1 %convert_subtract_fusion = bf16[1536,1536]{1,0:T(8,128)(2,1)} fusion(bf16[1,1536,1536]{2,1,0:T(8,128)(2,1)} %param.6, bf16[12288,512]{1,0:T(8,128)(2,1)} %bitcast.7, s32[]{:T(128)S(6)} %select_n.68, s32[]{:T(128)S(6)} %select_n.67), kind=kOutput, calls=%fused_computation.2 | convolution fusion | flops 2422996992 | bytes 12582920 | tf_op jit(solution)/shard_map/dot_general | solution.py:53
  302.2 5.6 %gather_fusion = bf16[6,256,1536]{2,1,0:T(8,128)(2,1)} fusion(bf16[6,256,1536]{2,1,0:T(8,128)(2,1)} %bitcast.25, s32[1024]{0:T(1024)S(1)} %get-tuple-element.13), kind=kCustom, calls=%fused_computation | custom fusion | bytes 9437208 | tf_op jit(solution)/shard_map/jit(_take)/gather | solution.py:64
  307.8 10.3 %gather.13 = bf16[1536,6,256]{2,1,0:T(8,128)(2,1)} reshape(bf16[6,256,1536]{2,1,0:T(8,128)(2,1)} %gather_fusion) | data formatting | bytes 9437184 | tf_op jit(solution)/shard_map/jit(_take)/gather | solution.py:64
  318.1 5.9 %copy_select_fusion = bf16[1536,6,256]{2,0,1:T(8,128)(2,1)} fusion(bf16[1536,6,256]{2,1,0:T(8,128)(2,1)} %gather.13, pred[1536]{0:T(1024)(128)(4,1)S(1)} %broadcast_in_dim.53), kind=kLoop, calls=%fused_computation.5 | loop fusion | flops 2359296 | bytes 9438720 | tf_op jit(solution)/shard_map/jit(_take)/select_n | solution.py:64
  323.9 5.5 %gather_fusion.1 = bf16[6,1536,256]{2,1,0:T(8,128)(2,1)} fusion(bf16[1536,6,256]{2,0,1:T(8,128)(2,1)} %copy_select_fusion, s32[1024]{0:T(1024)S(1)} %get-tuple-element.12), kind=kCustom, calls=%fused_computation.1 | custom fusion | bytes 9437208 | tf_op jit(solution)/shard_map/jit(_take)/gather | solution.py:65
  329.4 6.6 %copy.14 = bf16[1536,6,256]{0,2,1:T(8,128)(2,1)} copy(bf16[1536,6,256]{2,0,1:T(8,128)(2,1)} %bitcast.24) | data formatting | bytes 9437184 | tf_op jit(solution)/shard_map/jit(_take)/gather | solution.py:65
  336.0 3.2 fusion
  339.2 2.2 copy-done
  341.4 1.6 constant_dynamic-slice_fusion
  342.9 1.2 collective-permute-start
  344.1 2.8 copy.12
  347.0 48.3 %collective-permute-done = bf16[768,1536]{0,1:T(8,128)(2,1)} collective-permute-done((bf16[768,1536]{0,1:T(8,128)(2,1)}, bf16[768,1536]{0,1:T(8,128)(2,1)}, u32[]{:S(2)}, u32[]{:S(2)}) %collective-permute-start) | collective-permute-done | bytes 2359328 | tf_op jit(solution)/shard_map/ppermute | solution.py:16
  395.3 5.3 %fusion.2 = f32[1,768,1536]{1,2,0:T(8,128)} fusion(bf16[768,1536]{0,1:T(8,128)(2,1)} %collective-permute-done, bf16[1,768,1536]{1,2,0:T(8,128)(2,1)S(1)} %copy.12, bf16[1536,1536]{0,1:T(8,128)(2,1)} %copy-done, s32[]{:T(128)S(6)} %select_n.72), kind=kLoop, calls=%fused_computation.8 | loop fusion | flops 5898240 | bytes 11796484 | tf_op jit(solution)/shard_map/broadcast_in_dim | solution.py:77
  400.6 6.0 %copy.15 = f32[1,768,1536]{2,1,0:T(8,128)} copy(f32[1,768,1536]{1,2,0:T(8,128)} %fusion.2) | data formatting | bytes 9437184
  (10 shorter events, 0.1 us)
Async XLA Ops:
  2.9 6.0 %copy-start.1 = (bf16[192,512]{1,0:T(8,128)(2,1)}, bf16[192,512]{1,0:T(8,128)(2,1)S(1)}, u32[]{:S(2)}) copy-start(bf16[192,512]{1,0:T(8,128)(2,1)S(1)} %convolution_convert_fusion) | copy-start | bytes 589828
  8.9 11.4 %copy-start.2 = (s32[1,48]{1,0:T(1,128)S(1)}, s32[1,48]{1,0:T(1,128)}, u32[]{:S(2)}) copy-start(s32[1,48]{1,0:T(1,128)} %param.10) | copy-start | bytes 580
  8.9 285.2 %all-to-all-start = ((bf16[64,192,512]{2,1,0:T(8,128)(2,1)}), bf16[64,192,512]{2,1,0:T(8,128)(2,1)}, u32[]{:S(2)}, u32[]{:S(2)}) async-start(bf16[64,192,512]{2,1,0:T(8,128)(2,1)} %stack.2), calls=%async_computation | async-start | bytes 25165824 | tf_op jit(solution)/shard_map/all_to_all | solution.py:44
  339.2 2.2 copy-start
  342.9 52.4 %collective-permute-start = (bf16[768,1536]{0,1:T(8,128)(2,1)}, bf16[768,1536]{0,1:T(8,128)(2,1)}, u32[]{:S(2)}, u32[]{:S(2)}) collective-permute-start(bf16[768,1536]{0,1:T(8,128)(2,1)} %constant_dynamic-slice_fusion), channel_id=1, source_target_pairs={{0,64},{64,0},{128,192},{192,128},{1,65},{65,1},{129,193},{193,129... | collective-permute-start | bytes 7077896 | tf_op jit(solution)/shard_map/ppermute | solution.py:16
